TPU v7x, 32 devices: a whole 2x2x4 slice. The times are simulated.
32 devices in a mesh: dp: 8 (over z, y), tensor: 4 (over x, core).
Axes of the slice: x: 2, y: 2, z: 4, core: 2. Of those that a mesh axis runs over, the one named last changes fastest.
Arguments:
- query: bfloat16 [64, 64, 128], P('dp', 'tensor'), may hold values from -8 to 8
- kv_pages: bfloat16 [560, 8, 2, 128, 128], P('dp', 'tensor'), may hold values from -8 to 8
- move_plan: int32 [8, 3, 12], P('dp'), may hold values from 0 to 69, as said below
- move_count: int32 [8], P('dp'), may hold values from 9 to 12
- block_table: int32 [64, 8], P('dp'), may hold values from 0 to 69, as said below
- seq_lens: int32 [64], P('dp'), may hold values from 1 to 1024
- out_weight: bfloat16 [8192, 8192], P('tensor', 'dp'), may hold values from -0.0625 to 0.0625
Outputs:
- new_pages: bfloat16 [560, 8, 2, 128, 128], P('dp', 'tensor')
- projected: bfloat16 [64, 8192], P(None, 'dp')
Inputs may be any that keep to these rules, and one draw needn't show every extreme that they name: `move_plan`: row 0 holds the device's own source slots, distinct within a device; row 1 target devices; row 2 target slots. Entries at or past the device's move_count are padding to be ignored. At most 2 valid moves go from one device to one device, and some pair has exactly 2. The (target device, target slot) pairs of all valid moves are distinct. `block_table`: all entries of the sequences of one device are distinct slots of that device; sequence s belongs to device s // 8.
All inputs are finite; a program needn't handle non-finite values.
Results may differ from a plain program's by a relative error of at most 0.0055.
Values may be sent and summed in bfloat16 or wider, within the bound.
No kernel may reach another device: no remote copies, remote signals or barrier semaphores. Data moves between devices by JAX's collectives and lax.ppermute only.
A program may use at most 128 MiB of HBM per device.

v0:
```python
import math

import jax
import jax.numpy as jnp
from jax import lax
from jax.sharding import PartitionSpec as P

HD = 128
BLOCK = 128
BLOCKS = 8
CAP = 2


def body(query, kv_pages, move_plan, move_count, block_table, seq_lens, out_weight):
    slots_here = kv_pages.shape[0]
    move_total = move_plan.shape[2]
    devices = lax.axis_size("dp")
    capacity = CAP
    holding_rows = devices * capacity
    move_list = move_plan[0]
    move_index = jnp.arange(move_total, dtype=jnp.int32)
    is_valid = move_index < move_count[0]
    target_dev = move_list[1]
    earlier = (
        (target_dev[:, None] == target_dev[None, :])
        & is_valid[None, :]
        & (move_index[None, :] < move_index[:, None])
    )
    dest_rank = jnp.sum(earlier.astype(jnp.int32), axis=1)
    send_row = jnp.where(is_valid, target_dev * capacity + dest_rank, -1)
    flat_pages = kv_pages.reshape(slots_here, -1)
    picked = flat_pages[move_list[0]]
    select = jnp.arange(holding_rows, dtype=jnp.int32)[:, None] == send_row[None, :]
    outgoing = jnp.dot(
        select.astype(jnp.bfloat16), picked, preferred_element_type=jnp.float32
    ).astype(jnp.bfloat16)
    outgoing = outgoing.reshape((holding_rows,) + kv_pages.shape[1:])
    out_slots = jnp.sum(select.astype(jnp.int32) * (move_list[2][None, :] + 1), axis=1) - 1
    slot_tags = out_slots.astype(jnp.float32).astype(jnp.bfloat16)
    arrived, arrived_tags = (
        lax.all_to_all(outgoing, "dp", split_axis=0, concat_axis=0, tiled=True),
        lax.all_to_all(slot_tags, "dp", split_axis=0, concat_axis=0, tiled=True),
    )
    incoming = arrived_tags.astype(jnp.float32).astype(jnp.int32)
    hit_table = jnp.arange(slots_here, dtype=jnp.int32)[:, None] == incoming[None, :]
    placed = jnp.dot(
        hit_table.astype(jnp.bfloat16),
        arrived.reshape(holding_rows, -1),
        preferred_element_type=jnp.float32,
    ).astype(jnp.bfloat16)
    written = jnp.any(hit_table, axis=1)
    new_pages = jnp.where(written[:, None], placed, flat_pages).reshape(kv_pages.shape)
    seq_here = query.shape[0]
    local_heads = new_pages.shape[1]
    head_dim = query.shape[2]
    group_size = query.shape[1] // local_heads
    context = BLOCKS * BLOCK
    gathered = new_pages[block_table]
    key_rows = jnp.transpose(gathered[:, :, :, 0], (0, 2, 1, 3, 4)).reshape(
        seq_here, local_heads, context, head_dim
    )
    value_rows = jnp.transpose(gathered[:, :, :, 1], (0, 2, 1, 3, 4)).reshape(
        seq_here, local_heads, context, head_dim
    )
    grouped = query.reshape(seq_here, local_heads, group_size, head_dim)
    score_scale = 1.0 / math.sqrt(HD)
    scores = (
        jnp.einsum("skgd,sktd->skgt", grouped, key_rows, preferred_element_type=jnp.float32)
        * score_scale
    )
    position = jnp.arange(context, dtype=jnp.int32)
    scores = jnp.where(position[None, None, None, :] < seq_lens[:, None, None, None], scores, -1e30)
    largest = jnp.max(scores, axis=-1, keepdims=True)
    expo = jnp.exp(scores - largest)
    weights = (expo / jnp.sum(expo, axis=-1, keepdims=True)).astype(jnp.bfloat16)
    mixed_heads = jnp.einsum(
        "skgt,sktd->skgd", weights, value_rows, preferred_element_type=jnp.float32
    )
    attention = mixed_heads.reshape(seq_here, local_heads * group_size * head_dim).astype(
        jnp.bfloat16
    )
    partial_sums = jnp.dot(
        lax.all_gather(attention, "dp", axis=0, tiled=True),
        out_weight,
        preferred_element_type=jnp.float32,
    )
    summed = lax.psum(partial_sums, "tensor")
    return (new_pages, summed.astype(jnp.bfloat16))


def solution(mesh):
    placed = (
        P("dp", "tensor", None),
        P("dp", "tensor", None, None, None),
        P("dp", None, None),
        P("dp"),
        P("dp", None),
        P("dp"),
        P("tensor", "dp"),
    )
    return jax.shard_map(
        body,
        mesh=mesh,
        in_specs=placed,
        out_specs=(P("dp", "tensor", None, None, None), P(None, "dp")),
        check_vma=False,
    )
```

profile of v0, /device:TPU:0, one launch (start us, length us, event | category | flops | bytes accessed | tf_op | source)
XLA Modules:
  0.0 194.9 jit_solution(8297206147046076033)
XLA Ops:
  0.6 0.0 copy-start
  0.6 0.7 slice_bitcast_fusion
  2.0 0.2 convert_reduce_fusion
  2.2 0.7 add_select_fusion
  2.8 0.1 select_reduce_fusion
  3.0 0.7 convert_element_type.79
  3.7 7.3 %all-to-all-start = ((bf16[8,2,1]{1,2,0:T(2,128)(2,1)}), bf16[8,2,1]{1,2,0:T(2,128)(2,1)S(1)}, u32[]{:S(2)}, u32[]{:S(2)}) async-start(bf16[8,2,1]{1,2,0:T(2,128)(2,1)} %convert_element_type.79), calls=%async_computation | async-start | bytes 8192 | tf_op jit(solution)/shard_map/all_to_all | solution.py:42
  11.0 0.7 fusion.16
  11.6 8.8 %pad.2 = bf16[72,512,128]{2,1,0:T(8,128)(2,1)} pad(bf16[70,512,128]{2,1,0:T(8,128)(2,1)} %bitcast.69, bf16[]{:T(256)} %constant.38), padding=0_2x0_0x0_0 | pad | bytes 18612226
  20.4 13.8 %copy.21 = bf16[9,8,512,128]{3,1,2,0:T(8,128)(2,1)} copy(bf16[9,8,512,128]{3,2,1,0:T(8,128)(2,1)} %bitcast.62) | data formatting | bytes 18874368
  34.2 7.8 %gather_fusion = bf16[12,65536]{1,0:T(8,128)(2,1)S(1)} fusion(bf16[70,65536]{1,0:T(8,128)(2,1)} %bitcast.59, s32[1024]{0:T(1024)S(1)} %pad_clamp_fusion.1), kind=kCustom, calls=%fused_computation | custom fusion | bytes 3145776 | tf_op jit(solution)/shard_map/gather | solution.py:32
  42.1 0.7 fusion.4
  42.8 1.9 copy.22
  44.7 6.0 %all-to-all-start.1 = ((bf16[16,2,2,128,128]{4,3,2,1,0:T(8,128)(2,1)}), bf16[16,2,2,128,128]{4,3,2,1,0:T(8,128)(2,1)S(1)}, u32[]{:S(2)}, u32[]{:S(2)}) async-start(bf16[16,2,2,128,128]{4,3,2,1,0:T(8,128)(2,1)} %bitcast.24), calls=%async_computation.1 | async-start | bytes 4194304 | tf_op jit(solution)/shard_map/all_to_all | solution.py:41
  50.7 0.1 reshape.158
  50.8 0.1 iota_compare_fusion
  50.9 0.1 convert_element_type.72
  50.9 0.1 fusion.12
  51.0 47.3 %all-to-all-done.1 = bf16[16,2,2,128,128]{4,3,2,1,0:T(8,128)(2,1)S(1)} async-done(((bf16[16,2,2,128,128]{4,3,2,1,0:T(8,128)(2,1)}), bf16[16,2,2,128,128]{4,3,2,1,0:T(8,128)(2,1)S(1)}, u32[]{:S(2)}, u32[]{:S(2)}) %all-to-all-start.1) | async-done | bytes 2097184 | tf_op jit(solution)/shard_map/all_to_all | solution.py:41
  98.3 10.8 %fusion.1 = bf16[70,65536]{1,0:T(8,128)(2,1)} fusion(bf16[70,65536]{1,0:T(8,128)(2,1)} %bitcast.60, pred[70]{0:T(512)(128)(4,1)S(1)} %fusion.12, bf16[2,8,512,128]{3,2,1,0:T(8,128)(2,1)S(1)} %bitcast.70, s32[16]{0:T(128)S(1)} %convert_element_type.72), kind=kOutput, calls=%fused_computation.4 | convolution fusion | flops 155976800 | bytes 20447366 | tf_op jit(solution)/shard_map/dot_general | solution.py:46
  109.1 9.9 %copy.24 = bf16[9,8,512,128]{3,2,1,0:T(8,128)(2,1)} copy(bf16[9,8,512,128]{3,1,2,0:T(8,128)(2,1)} %bitcast.61) | data formatting | bytes 18874368
  119.0 8.4 %slice.29 = bf16[70,512,128]{2,1,0:T(8,128)(2,1)} slice(bf16[72,512,128]{2,1,0:T(8,128)(2,1)} %bitcast.63), slice={[0:70], [0:512], [0:128]} | slice | bytes 18350080
  127.4 9.1 %gather_fusion.1 = bf16[64,2,2,128,128]{4,3,2,1,0:T(8,128)(2,1)} fusion(bf16[70,2,2,128,128]{4,3,2,1,0:T(8,128)(2,1)} %bitcast.64, s32[1024]{0:T(1024)S(1)} %pad_clamp_fusion), kind=kCustom, calls=%fused_computation.1 | custom fusion | bytes 16777472 | tf_op jit(solution)/shard_map/gather | solution.py:58
  136.5 3.8 %fusion.17 = (bf16[8,8,2,1,128,128]{5,4,3,2,1,0:T(8,128)(2,1)S(1)}, bf16[8,8,2,1,128,128]{5,4,3,2,1,0:T(8,128)(2,1)S(1)}) fusion(bf16[8,8,2,2,128,128]{5,4,3,2,1,0:T(8,128)(2,1)} %bitcast.66), kind=kLoop, calls=%fused_computation.41 | loop fusion | bytes 16777216 | tf_op jit(solution)/shard_map/slice | solution.py:59
  140.4 0.6 copy.19
  140.9 1.2 fusion.8
  142.1 0.3 fusion.18
  142.4 2.2 %copy.20 = bf16[8,8,2,1,128,128]{5,4,1,2,0,3:T(8,128)(2,1)} copy(bf16[8,8,2,1,128,128]{5,4,3,2,1,0:T(8,128)(2,1)S(1)} %get-tuple-element.3) | data formatting | bytes 8388608
  144.6 2.9 %fusion.9 = bf16[1,8,16,128]{3,2,1,0:T(8,128)(2,1)S(1)} fusion(bf16[8,2,1024,128]{3,2,1,0:T(8,128)(2,1)} %bitcast.67, f32[8,2,8]{2,1,0:T(2,128)S(1)} %fusion.18, f32[8,2,8,1024]{3,2,1,0:T(8,128)S(1)} %fusion.8), kind=kOutput, calls=%fused_computation.15 | convolution fusion | flops 33965184 | bytes 4751872 | tf_op jit(solution)/shard_map/skgt,sktd->skgd/dot_general | solution.py:76
  147.6 30.8 %all_gather.3 = bf16[64,2048]{1,0:T(8,128)(2,1)S(1)} all-gather(bf16[8,2048]{1,0:T(8,128)(2,1)S(1)} %bitcast.71), channel_id=1, replica_groups=mesh['dp'=8,'tensor'=4] {'dp'}, dimensions={0}, use_global_device_ids=true | all-gather | bytes 294912 | tf_op jit(solution)/shard_map/all_gather | solution.py:83
  178.3 3.0 %fusion.19 = f32[64,1024]{1,0:T(8,128)S(1)} fusion(bf16[64,2048]{1,0:T(8,128)(2,1)S(1)} %all_gather.3, bf16[2048,1024]{1,0:T(8,128)(2,1)} %param.13), kind=kOutput, calls=%fused_computation.43 | convolution fusion | flops 268435456 | bytes 4718592 | tf_op jit(solution)/shard_map/dot_general | solution.py:82
  181.4 13.5 %all-reduce.1 = bf16[64,1024]{1,0:T(8,128)(2,1)} all-reduce(f32[64,1024]{1,0:T(8,128)S(1)} %fusion.19), channel_id=1, replica_groups=mesh['dp'=8,'tensor'=4] {'tensor'}, use_global_device_ids=true, to_apply=%region_5.6 | all-reduce | flops 65536 | bytes 393216 | tf_op jit(solution)/shard_map/psum | solution.py:87
  (13 shorter events, 0.1 us)
Async XLA Ops:
  0.6 140.3 %copy-start = (bf16[8,16,128]{2,1,0:T(8,128)(2,1)S(1)}, bf16[8,16,128]{2,1,0:T(8,128)(2,1)}, u32[]{:S(2)}) copy-start(bf16[8,16,128]{2,1,0:T(8,128)(2,1)} %param.7) | copy-start | bytes 98308
  3.7 41.0 %all-to-all-start = ((bf16[8,2,1]{1,2,0:T(2,128)(2,1)}), bf16[8,2,1]{1,2,0:T(2,128)(2,1)S(1)}, u32[]{:S(2)}, u32[]{:S(2)}) async-start(bf16[8,2,1]{1,2,0:T(2,128)(2,1)} %convert_element_type.79), calls=%async_computation | async-start | bytes 8192 | tf_op jit(solution)/shard_map/all_to_all | solution.py:42
  42.7 7.9 %copy-start.1 = (s32[8,8]{1,0:T(8,128)S(1)}, s32[8,8]{1,0:T(8,128)}, u32[]{:S(2)}) copy-start(s32[8,8]{1,0:T(8,128)} %param.11) | copy-start | bytes 772
  42.8 8.0 %copy-start.2 = (s32[8]{0:T(128)S(1)}, s32[8]{0:T(128)}, u32[]{:S(2)}) copy-start(s32[8]{0:T(128)} %param.12) | copy-start | bytes 100
  44.7 53.7 %all-to-all-start.1 = ((bf16[16,2,2,128,128]{4,3,2,1,0:T(8,128)(2,1)}), bf16[16,2,2,128,128]{4,3,2,1,0:T(8,128)(2,1)S(1)}, u32[]{:S(2)}, u32[]{:S(2)}) async-start(bf16[16,2,2,128,128]{4,3,2,1,0:T(8,128)(2,1)} %bitcast.24), calls=%async_computation.1 | async-start | bytes 4194304 | tf_op jit(solution)/shard_map/all_to_all | solution.py:41
where the time goes:
time: 196 us; the launch traced here: 195 us
  local copies, waits for them, and re-layouts  67.2 us (34%)
  waiting for transfers between devices  47.3 us (24%)
  blocking collectives  44.2 us (23%)
  matrix products  18.6 us (9%)
  starting transfers between devices  13.3 us (7%)
  other arithmetic  2.78 us (1%)
    all_to_all x1, waiting for transfers between devices, body(): lax.all_to_all(outgoing, 'dp', split_axis=0, concat_axis=0, tiled=True)  47.3 us
    unnamed x14, local copies, waits for them, and re-layouts  45.6 us
    all_gather x1, blocking collectives, body(): lax.all_gather(attention, 'dp', axis=0, tiled=True)  30.8 us
    psum x1, blocking collectives, body(): summed = lax.psum(partial_sums, 'tensor')  13.5 us
    dot_general x1, matrix products, body(): jnp.dot(hit_table.astype(jnp.bfloat16), arrived.reshape(holding_rows, -1)...  10.8 us
    gather x1, local copies, waits for them, and re-layouts, body(): gathered = new_pages[block_table]  9.14 us
    gather x1, local copies, waits for them, and re-layouts, body(): picked = flat_pages[move_list[0]]  7.81 us
    all_to_all x1, starting transfers between devices, body(): lax.all_to_all(slot_tags, 'dp', split_axis=0, concat_axis=0, tiled=True)  7.31 us
  transfers between devices with their start and end apart: 2, of which 1 were waited for; matrix products, arithmetic and copies ran while one was open for 17% of the time, Pallas kernels for 0%

commit v1 on v0

v1 whole, which is shorter than its diff:
```python
import functools
import math

import jax
import jax.numpy as jnp
from jax import lax
from jax.experimental import pallas as pl
from jax.experimental.pallas import tpu as pltpu
from jax.sharding import PartitionSpec as P

CAP = 2
ROW = 8
NEG = -1e30

ANY = pl.BlockSpec(memory_space=pl.ANY)
VMEM = pl.BlockSpec(memory_space=pltpu.VMEM)
SMEM = pl.BlockSpec(memory_space=pltpu.SMEM)


def pack_kernel(plan, count, pages, out, used, tags, sem):
    devices = out.shape[0]
    rows = pages.shape[1]
    moves = plan.shape[1]
    for d in range(devices):
        used[d] = 0
        for r in range(CAP):
            tags[d * CAP + r] = -1

    def page_copy(source, target, rank):
        place = pl.ds(pl.multiple_of(rank * rows, rows), rows)
        return pltpu.make_async_copy(pages.at[source], out.at[target, place], sem)

    def send(k, carry):
        @pl.when(k < count[0])
        def _():
            target = plan[1, k]
            rank = used[target]
            used[target] = rank + 1
            tags[target * CAP + rank] = plan[2, k]
            page_copy(plan[0, k], target, rank).start()

        return carry

    lax.fori_loop(0, moves, send, 0)
    row_at = lax.broadcasted_iota(jnp.int32, (ROW, pages.shape[2]), 0)
    for d in range(devices):
        tile = jnp.full(row_at.shape, -1, jnp.int32)
        for r in range(CAP):
            tile = jnp.where(row_at == r, tags[d * CAP + r], tile)
        out[d, CAP * rows :] = tile.astype(jnp.float32).astype(out.dtype)

    def finish(k, carry):
        @pl.when(k < count[0])
        def _():
            page_copy(0, 0, 0).wait()

        return carry

    lax.fori_loop(0, moves, finish, 0)


def page_partial(q8, key_page, value_page, first, length, scale):
    scores = (
        lax.dot_general(
            q8, key_page, (((1,), (1,)), ((), ())), preferred_element_type=jnp.float32
        )
        * scale
    )
    position = first + lax.broadcasted_iota(jnp.int32, scores.shape, 1)
    scores = jnp.where(position < length, scores, NEG)
    largest = jnp.max(scores, axis=1, keepdims=True)
    expo = jnp.exp(scores - largest)
    total = jnp.sum(expo, axis=1, keepdims=True)
    mixed = jnp.dot(
        expo.astype(jnp.bfloat16), value_page, preferred_element_type=jnp.float32
    )
    return largest, total, mixed


def local_kernel(
    heads, scale, table, lens, query, pages, new_pages, mixed_out, stat_out, owner,
    held, read_sem, write_sem,
):
    slots = pages.shape[0]
    block = pages.shape[1] // (2 * heads)
    seqs, blocks = table.shape
    group = query.shape[1] // heads
    lanes = query.shape[2]

    def read(i):
        return pltpu.make_async_copy(pages.at[i], held.at[i], read_sem.at[i])

    def write(i):
        return pltpu.make_async_copy(held.at[i], new_pages.at[i], write_sem)

    def start_read(i, carry):
        read(i).start()
        owner[i] = -1
        return carry

    lax.fori_loop(0, slots, start_read, 0)

    def own(i, carry):
        for b in range(blocks):
            owner[table[i, b]] = i * blocks + b
        return carry

    lax.fori_loop(0, seqs, own, 0)

    def pass_on(i, carry):
        read(i).wait()
        write(i).start()
        return carry

    lax.fori_loop(0, slots, pass_on, 0)
    lane_at = lax.broadcasted_iota(jnp.int32, (group, lanes), 1)

    def sequence(i, carry):
        length = lens[i]
        q_rows = query[i].astype(jnp.float32)
        for b in range(blocks):
            slot = table[i, b]
            for h in range(heads):
                q8 = q_rows[h * group : (h + 1) * group].astype(jnp.bfloat16)
                top = 2 * h * block
                largest, total, mixed = page_partial(
                    q8,
                    held[slot, top : top + block],
                    held[slot, top + block : top + 2 * block],
                    b * block,
                    length,
                    scale,
                )
                mixed_out[i, b, h] = mixed
                stat_out[i, b, h] = jnp.where(lane_at < lanes // 2, largest, total)
        return carry

    lax.fori_loop(0, seqs, sequence, 0)

    def finish(i, carry):
        write(i).wait()
        return carry

    lax.fori_loop(0, slots, finish, 0)


def final_kernel(
    heads, scale, copies, lens, owner, query, arrived, mixed_in, stat_in, pages_in,
    pages_out, out, mixed, stat, tags, sem, in_sem,
):
    devices = arrived.shape[0]
    rows = pages_out.shape[1]
    block = rows // (2 * heads)
    seqs = query.shape[0]
    blocks = mixed_in.shape[1]
    group = query.shape[1] // heads
    lanes = query.shape[2]
    fetch = [
        pltpu.make_async_copy(mixed_in, mixed, in_sem.at[0]),
        pltpu.make_async_copy(stat_in, stat, in_sem.at[1]),
    ]
    for copy in fetch:
        copy.start()

    row_at = lax.broadcasted_iota(jnp.int32, (ROW, lanes), 0)
    for d in range(devices):
        tile = arrived[d, CAP * rows :].astype(jnp.float32)
        for r in range(CAP):
            tags[d * CAP + r] = jnp.max(jnp.where(row_at == r, tile, -1.0)).astype(jnp.int32)

    def place(d, r, slot):
        return pltpu.make_async_copy(
            arrived.at[d, pl.ds(r * rows, rows)], pages_out.at[slot], sem
        )

    for d in range(devices):
        for r in range(CAP):
            @pl.when(tags[d * CAP + r] >= 0)
            def _():
                place(d, r, tags[d * CAP + r]).start()

    for copy in fetch:
        copy.wait()
    lane_at = lax.broadcasted_iota(jnp.int32, (group, lanes), 1)

    def renew(d):
        for r in range(CAP):
            slot = tags[d * CAP + r]
            entry = jnp.where(slot >= 0, owner[jnp.maximum(slot, 0)], -1)
            at = jnp.maximum(entry, 0)
            i = at // blocks
            b = at - i * blocks
            q_rows = query[i].astype(jnp.float32)
            found = []
            for h in range(heads):
                q8 = q_rows[h * group : (h + 1) * group].astype(jnp.bfloat16)
                top = r * rows + 2 * h * block
                found.append(
                    page_partial(
                        q8,
                        arrived[d, top : top + block],
                        arrived[d, top + block : top + 2 * block],
                        b * block,
                        lens[i],
                        scale,
                    )
                )

            @pl.when(entry >= 0)
            def _():
                for h, (largest, total, part) in enumerate(found):
                    mixed[i, b, h] = part
                    stat[i, b, h] = jnp.where(lane_at < lanes // 2, largest, total)

    if devices <= 8:
        for d in range(devices):
            renew(d)
    else:
        lax.fori_loop(0, devices, lambda d, c: (renew(d), c)[1], 0)

    for h in range(heads):
        for i in range(seqs):
            stats = stat[i, :, h]
            largest = stats[:, :, :1]
            total = stats[:, :, lanes // 2 : lanes // 2 + 1]
            top = jnp.max(largest, axis=0, keepdims=True)
            factor = jnp.exp(largest - top)
            weight = factor / jnp.sum(factor * total, axis=0, keepdims=True)
            value = jnp.sum(mixed[i, :, h] * weight, axis=0).astype(out.dtype)
            for c in range(copies):
                out[c, i, h * group : (h + 1) * group] = value

    for d in range(devices):
        for r in range(CAP):
            @pl.when(tags[d * CAP + r] >= 0)
            def _():
                place(d, r, 0).wait()


def exchange_sum(value, size):
    me = lax.axis_index("tensor")
    pairs = lambda bit: [(i, i ^ bit) for i in range(size)]
    half = value.shape[0] // 2
    low = (me % 2) == 0
    travel = value.astype(jnp.bfloat16)
    given = jnp.where(low, travel[half:], travel[:half])
    kept = jnp.where(low, value[:half], value[half:])
    total = kept + lax.ppermute(given, "tensor", pairs(1)).astype(jnp.float32)
    bit = 2
    while bit < size:
        total = total + lax.ppermute(
            total.astype(jnp.bfloat16), "tensor", pairs(bit)
        ).astype(jnp.float32)
        bit *= 2
    mine = total.astype(jnp.bfloat16)
    other = lax.ppermute(mine, "tensor", pairs(1))
    return jnp.concatenate([jnp.where(low, mine, other), jnp.where(low, other, mine)])


def body(query, kv_pages, move_plan, move_count, block_table, seq_lens, out_weight):
    slots, heads, two, block, lanes = kv_pages.shape
    seqs, local_q, _ = query.shape
    devices = lax.axis_size("dp")
    tensor = lax.axis_size("tensor")
    blocks = block_table.shape[1]
    group = local_q // heads
    rows = heads * two * block
    scale = 1.0 / math.sqrt(lanes)
    pages = kv_pages.reshape(slots, rows, lanes)
    plan = move_plan.reshape(move_plan.shape[1:])

    outgoing = pl.pallas_call(
        pack_kernel,
        out_shape=jax.ShapeDtypeStruct((devices, CAP * rows + ROW, lanes), kv_pages.dtype),
        in_specs=[SMEM, SMEM, ANY],
        out_specs=VMEM,
        scratch_shapes=[
            pltpu.SMEM((devices,), jnp.int32),
            pltpu.SMEM((devices * CAP,), jnp.int32),
            pltpu.SemaphoreType.DMA,
        ],
        name="pack",
    )(plan, move_count, pages)
    arrived = lax.all_to_all(outgoing, "dp", split_axis=0, concat_axis=0, tiled=True)

    part_shape = jax.ShapeDtypeStruct((seqs, blocks, heads, group, lanes), jnp.float32)
    copied, mixed, stat, owner = pl.pallas_call(
        functools.partial(local_kernel, heads, scale),
        out_shape=(
            jax.ShapeDtypeStruct(pages.shape, pages.dtype),
            part_shape,
            part_shape,
            jax.ShapeDtypeStruct((slots,), jnp.int32),
        ),
        in_specs=[SMEM, SMEM, VMEM, ANY],
        out_specs=(ANY, VMEM, VMEM, SMEM),
        scratch_shapes=[
            pltpu.VMEM(pages.shape, pages.dtype),
            pltpu.SemaphoreType.DMA((slots,)),
            pltpu.SemaphoreType.DMA,
        ],
        name="local",
        cost_estimate=pl.CostEstimate(
            flops=4 * seqs * blocks * local_q * block * lanes,
            bytes_accessed=4 * slots * rows * lanes,
            transcendentals=0,
        ),
    )(block_table, seq_lens, query, pages)

    new_pages, attention = pl.pallas_call(
        functools.partial(final_kernel, heads, scale, devices),
        out_shape=(
            jax.ShapeDtypeStruct(pages.shape, pages.dtype),
            jax.ShapeDtypeStruct((devices, seqs, local_q, lanes), jnp.bfloat16),
        ),
        in_specs=[SMEM, SMEM, VMEM, VMEM, ANY, ANY, ANY],
        out_specs=(ANY, VMEM),
        scratch_shapes=[
            pltpu.VMEM(part_shape.shape, jnp.float32),
            pltpu.VMEM(part_shape.shape, jnp.float32),
            pltpu.SMEM((devices * CAP,), jnp.int32),
            pltpu.SemaphoreType.DMA,
            pltpu.SemaphoreType.DMA((2,)),
        ],
        input_output_aliases={6: 0},
        name="final",
    )(seq_lens, owner, query, arrived, mixed, stat, copied)

    every = lax.all_to_all(attention, "dp", split_axis=0, concat_axis=0, tiled=True)
    partial_sums = jnp.dot(
        every.reshape(devices * seqs, local_q * lanes),
        out_weight,
        preferred_element_type=jnp.float32,
    )
    summed = exchange_sum(partial_sums, tensor)
    return (new_pages.reshape(kv_pages.shape), summed)


def solution(mesh):
    placed = (
        P("dp", "tensor", None),
        P("dp", "tensor", None, None, None),
        P("dp", None, None),
        P("dp"),
        P("dp", None),
        P("dp"),
        P("tensor", "dp"),
    )
    return jax.shard_map(
        body,
        mesh=mesh,
        in_specs=placed,
        out_specs=(P("dp", "tensor", None, None, None), P(None, "dp")),
        check_vma=False,
    )
```

time: 196 us -> 102 us (0.52)
  local copies, waits for them, and re-layouts: 67.2 us -> 2.59 us
  Pallas kernels: 0 us -> 57.5 us
  blocking collectives: 44.2 us -> 0 us
  waiting for transfers between devices: 47.3 us -> 23.2 us
  matrix products: 18.6 us -> 3.03 us
  other arithmetic: 2.78 us -> 0.75 us
    pallas_call x0 -> x3, Pallas kernels: none -> 57.5 us  [the longest x1 39.7 us: body(): pl.pallas_call(functools.partial(local_kernel, heads, scale), out_shape=(...]
    unnamed x14 -> x3, local copies, waits for them, and re-layouts: 45.6 us -> 2.59 us
    all_to_all x1, waiting for transfers between devices: 47.3 us -> 8.84 us  [body(): lax.all_to_all(outgoing, 'dp', split_axis=0, concat_axis=0, tiled=True)]
    all_gather x1 -> x0, blocking collectives: 30.8 us -> none  [body(): lax.all_gather(attention, 'dp', axis=0, tiled=True)]
    gather x2 -> x0, local copies, waits for them, and re-layouts: 16.9 us -> none  [the longest x1 9.14 us: body(): gathered = new_pages[block_table]]
    dot_general x5 -> x1, matrix products: 18.6 us -> 3.03 us  [body(): jnp.dot(every.reshape(devices * seqs, local_q * lanes), out_weight, prefe...]
    psum x1 -> x0, blocking collectives: 13.5 us -> none  [body(): summed = lax.psum(partial_sums, 'tensor')]
    all_to_all x1, waiting for transfers between devices: 0.01 us -> 9.1 us  [body(): lax.all_to_all(attention, 'dp', split_axis=0, concat_axis=0, tiled=True)]
  transfers between devices with their start and end apart: 2 -> 5, of which waited for: 1 -> 5; matrix products, arithmetic and copies ran while one was open for 17% -> 0% of each run, Pallas kernels for 0% -> 39%
where the time goes in v1:
time: 102 us; the launch traced here: 101 us
  Pallas kernels  57.5 us (56%)
  waiting for transfers between devices  23.2 us (23%)
  starting transfers between devices  12.7 us (12%)
  matrix products  3.03 us (3%)
  local copies, waits for them, and re-layouts  2.59 us (3%)
  between operations  1.35 us (1%)
    pallas_call x1, Pallas kernels, body(): pl.pallas_call(functools.partial(local_kernel, heads, scale), out_shape=(...  39.7 us
    pallas_call x1, Pallas kernels, body(): pl.pallas_call(functools.partial(final_kernel, heads, scale, devices), ou...  14.3 us
    all_to_all x1, waiting for transfers between devices, body(): lax.all_to_all(attention, 'dp', split_axis=0, concat_axis=0, tiled=True)  9.1 us
    all_to_all x1, waiting for transfers between devices, body(): lax.all_to_all(outgoing, 'dp', split_axis=0, concat_axis=0, tiled=True)  8.84 us
    all_to_all x1, starting transfers between devices, body(): lax.all_to_all(outgoing, 'dp', split_axis=0, concat_axis=0, tiled=True)  7.32 us
    all_to_all x1, starting transfers between devices, body(): lax.all_to_all(attention, 'dp', split_axis=0, concat_axis=0, tiled=True)  3.64 us
    pallas_call x1, Pallas kernels, body(): pl.pallas_call(pack_kernel, out_shape=jax.ShapeDtypeStruct((devices, CAP...  3.46 us
    dot_general x1, matrix products, body(): jnp.dot(every.reshape(devices * seqs, local_q * lanes), out_weight, prefe...  3.03 us
  transfers between devices with their start and end apart: 5, of which 5 were waited for; matrix products, arithmetic and copies ran while one was open for 0% of the time, Pallas kernels for 39%

profile of v1, /device:TPU:0, one launch (start us, length us, event | category | flops | bytes accessed | tf_op | source)
XLA Modules:
  0.0 101.0 jit_solution(8635551338908604149)
XLA Ops:
  0.6 1.3 %copy.19 = s32[1,3,12]{2,1,0:T(4,128)} copy(s32[1,3,12]{2,0,1:T(1,128)} %param.9) | data formatting | bytes 288
  2.5 3.5 %pack.1 = bf16[8,1032,128]{2,1,0:T(8,128)(2,1)} custom-call(s32[3,12]{1,0:T(4,128)} %bitcast.16, s32[1]{0:T(128)S(6)} %copy.21.count, bf16[70,512,128]{2,1,0:T(8,128)(2,1)} %bitcast.13), custom_call_target="tpu_custom_call" | custom-call | tf_op jit(solution)/shard_map/pack/pallas_call | solution.py:272
  6.0 7.3 %all-to-all-start = ((bf16[8,1032,128]{2,1,0:T(8,128)(2,1)}), bf16[8,1032,128]{2,1,0:T(8,128)(2,1)S(1)}, u32[]{:S(2)}, u32[]{:S(2)}) async-start(bf16[8,1032,128]{2,1,0:T(8,128)(2,1)} %pack.1), calls=%async_computation | async-start | bytes 4227072 | tf_op jit(solution)/shard_map/all_to_all | solution.py:284
  13.3 39.7 %local.1 = (bf16[70,512,128]{2,1,0:T(8,128)(2,1)}, f32[8,8,2,8,128]{4,3,2,1,0:T(8,128)}, f32[8,8,2,8,128]{4,3,2,1,0:T(8,128)}, s32[70]{0:T(128)}) custom-call(s32[8,8]{1,0:T(8,128)} %table.1, s32[8]{0:T(128)} %lens.3, bf16[8,16,128]{2,1,0:T(8,128)(2,1)} %query.3, bf16[70,512,128]{2,1,0:T(8,128)(2,1)} %bitcast.14), custom_call_target="tpu_custom_call" | custom-call | flops 67108864 | bytes 18350080 | tf_op jit(solution)/shard_map/local/pallas_call | solution.py:287
  53.1 8.8 %all-to-all-done.arrived = bf16[8,1032,128]{2,1,0:T(8,128)(2,1)S(1)} async-done(((bf16[8,1032,128]{2,1,0:T(8,128)(2,1)}), bf16[8,1032,128]{2,1,0:T(8,128)(2,1)S(1)}, u32[]{:S(2)}, u32[]{:S(2)}) %all-to-all-start) | async-done | bytes 2113568 | tf_op jit(solution)/shard_map/all_to_all | solution.py:284
  61.9 0.0 copy-start
  61.9 1.3 %copy-done = bf16[8,1032,128]{2,1,0:T(8,128)(2,1)} copy-done((bf16[8,1032,128]{2,1,0:T(8,128)(2,1)}, bf16[8,1032,128]{2,1,0:T(8,128)(2,1)S(1)}, u32[]{:S(2)}) %copy-start) | copy-done | bytes 2113560
  63.3 14.3 %final.1 = (bf16[70,512,128]{2,1,0:T(8,128)(2,1)}, bf16[8,8,16,128]{3,2,1,0:T(8,128)(2,1)}) custom-call(s32[8]{0:T(128)} %lens.3, s32[70]{0:T(128)} %get-tuple-element.8.owner, bf16[8,16,128]{2,1,0:T(8,128)(2,1)} %query.3, bf16[8,1032,128]{2,1,0:T(8,128)(2,1)} %copy-done, ...), custom_call_target="tpu_custom_call", output_to_operand_aliasing={{0}: (6, {})} | custom-call | tf_op jit(solution)/shard_map/final/pallas_call | solution.py:310
  77.5 3.6 %all-to-all-start.1 = ((bf16[8,8,16,128]{3,2,1,0:T(8,128)(2,1)}), bf16[8,8,16,128]{3,2,1,0:T(8,128)(2,1)S(1)}, u32[]{:S(2)}, u32[]{:S(2)}) async-start(bf16[8,8,16,128]{3,2,1,0:T(8,128)(2,1)} %get-tuple-element.13), calls=%async_computation.1 | async-start | bytes 524288 | tf_op jit(solution)/shard_map/all_to_all | solution.py:329
  81.2 9.1 %all-to-all-done.1 = bf16[8,8,16,128]{3,2,1,0:T(8,128)(2,1)S(1)} async-done(((bf16[8,8,16,128]{3,2,1,0:T(8,128)(2,1)}), bf16[8,8,16,128]{3,2,1,0:T(8,128)(2,1)S(1)}, u32[]{:S(2)}, u32[]{:S(2)}) %all-to-all-start.1) | async-done | bytes 262176 | tf_op jit(solution)/shard_map/all_to_all | solution.py:329
  90.3 3.0 %fusion.5 = (bf16[64,1024]{1,0:T(8,128)(2,1)S(1)}, f32[64,1024]{1,0:T(8,128)S(1)}) fusion(bf16[2048,1024]{1,0:T(8,128)(2,1)} %param.13, bf16[8,8,16,128]{3,2,1,0:T(8,128)(2,1)S(1)} %all-to-all-done.1), kind=kOutput, calls=%fused_computation.12 | convolution fusion | flops 268500992 | bytes 4849664 | tf_op jit(solution)/shard_map/dot_general | solution.py:330
  93.3 0.1 collective-permute-start
  93.4 1.2 %collective-permute-done = bf16[32,1024]{1,0:T(8,128)(2,1)S(1)} collective-permute-done((bf16[32,1024]{1,0:T(8,128)(2,1)S(1)}, bf16[32,1024]{1,0:T(8,128)(2,1)S(1)}, u32[]{:S(2)}, u32[]{:S(2)}) %collective-permute-start) | collective-permute-done | bytes 65568 | tf_op jit(solution)/shard_map/ppermute | solution.py:248
  94.7 1.6 %collective-permute-start.1 = (bf16[32,1024]{1,0:T(8,128)(2,1)S(1)}, bf16[32,1024]{1,0:T(8,128)(2,1)S(1)}, u32[]{:S(2)}, u32[]{:S(2)}) collective-permute-start(bf16[32,1024]{1,0:T(8,128)(2,1)S(1)} %fusion.4), channel_id=1, source_target_pairs={{0,2},{1,3},{2,0},{3,1},{4,6},{5,7},{6,4},{7,5},{8,10},{9,11},{10,... | collective-permute-start | bytes 196616 | tf_op jit(solution)/shard_map/ppermute | solution.py:251
  96.2 2.8 %collective-permute-done.1 = bf16[32,1024]{1,0:T(8,128)(2,1)S(1)} collective-permute-done((bf16[32,1024]{1,0:T(8,128)(2,1)S(1)}, bf16[32,1024]{1,0:T(8,128)(2,1)S(1)}, u32[]{:S(2)}, u32[]{:S(2)}) %collective-permute-start.1) | collective-permute-done | bytes 65568 | tf_op jit(solution)/shard_map/ppermute | solution.py:251
  99.0 0.1 collective-permute-start.2
  99.1 1.2 %collective-permute-done.2 = bf16[32,1024]{1,0:T(8,128)(2,1)S(1)} collective-permute-done((bf16[32,1024]{1,0:T(8,128)(2,1)S(1)}, bf16[32,1024]{1,0:T(8,128)(2,1)S(1)}, u32[]{:S(2)}, u32[]{:S(2)}) %collective-permute-start.2) | collective-permute-done | bytes 65568 | tf_op jit(solution)/shard_map/ppermute | solution.py:256
  100.4 0.7 pad_maximum_fusion
  (4 shorter events, 0.1 us)
Async XLA Ops:
  6.0 55.9 %all-to-all-start = ((bf16[8,1032,128]{2,1,0:T(8,128)(2,1)}), bf16[8,1032,128]{2,1,0:T(8,128)(2,1)S(1)}, u32[]{:S(2)}, u32[]{:S(2)}) async-start(bf16[8,1032,128]{2,1,0:T(8,128)(2,1)} %pack.1), calls=%async_computation | async-start | bytes 4227072 | tf_op jit(solution)/shard_map/all_to_all | solution.py:284
  61.9 1.3 %copy-start = (bf16[8,1032,128]{2,1,0:T(8,128)(2,1)}, bf16[8,1032,128]{2,1,0:T(8,128)(2,1)S(1)}, u32[]{:S(2)}) copy-start(bf16[8,1032,128]{2,1,0:T(8,128)(2,1)S(1)} %all-to-all-done.arrived) | copy-start | bytes 6340612
  77.5 12.7 %all-to-all-start.1 = ((bf16[8,8,16,128]{3,2,1,0:T(8,128)(2,1)}), bf16[8,8,16,128]{3,2,1,0:T(8,128)(2,1)S(1)}, u32[]{:S(2)}, u32[]{:S(2)}) async-start(bf16[8,8,16,128]{3,2,1,0:T(8,128)(2,1)} %get-tuple-element.13), calls=%async_computation.1 | async-start | bytes 524288 | tf_op jit(solution)/shard_map/all_to_all | solution.py:329
  93.3 1.3 %collective-permute-start = (bf16[32,1024]{1,0:T(8,128)(2,1)S(1)}, bf16[32,1024]{1,0:T(8,128)(2,1)S(1)}, u32[]{:S(2)}, u32[]{:S(2)}) collective-permute-start(bf16[32,1024]{1,0:T(8,128)(2,1)S(1)} %slice_select_fusion.1), channel_id=1, source_target_pairs={{0,1},{1,0},{2,3},{3,2},{4,5},{5,4},{6,7},{7,6},{8,9},{9,8},{10,11... | collective-permute-start | bytes 196616 | tf_op jit(solution)/shard_map/ppermute | solution.py:248
  94.7 4.3 %collective-permute-start.1 = (bf16[32,1024]{1,0:T(8,128)(2,1)S(1)}, bf16[32,1024]{1,0:T(8,128)(2,1)S(1)}, u32[]{:S(2)}, u32[]{:S(2)}) collective-permute-start(bf16[32,1024]{1,0:T(8,128)(2,1)S(1)} %fusion.4), channel_id=1, source_target_pairs={{0,2},{1,3},{2,0},{3,1},{4,6},{5,7},{6,4},{7,5},{8,10},{9,11},{10,... | collective-permute-start | bytes 196616 | tf_op jit(solution)/shard_map/ppermute | solution.py:251
  99.0 1.3 %collective-permute-start.2 = (bf16[32,1024]{1,0:T(8,128)(2,1)S(1)}, bf16[32,1024]{1,0:T(8,128)(2,1)S(1)}, u32[]{:S(2)}, u32[]{:S(2)}) collective-permute-start(bf16[32,1024]{1,0:T(8,128)(2,1)S(1)} %add_convert_fusion), channel_id=1, source_target_pairs={{0,1},{1,0},{2,3},{3,2},{4,5},{5,4},{6,7},{7,6},{8,9},{9,8},{10,11... | collective-permute-start | bytes 196616 | tf_op jit(solution)/shard_map/ppermute | solution.py:256

commit v2 on v1

v2 whole, which is shorter than its diff:
```python
import functools
import math

import jax
import jax.numpy as jnp
from jax import lax
from jax.experimental import pallas as pl
from jax.experimental.pallas import tpu as pltpu
from jax.sharding import PartitionSpec as P

CAP = 2
ROW = 8
NEG = -1e30

ANY = pl.BlockSpec(memory_space=pl.ANY)
VMEM = pl.BlockSpec(memory_space=pltpu.VMEM)
SMEM = pl.BlockSpec(memory_space=pltpu.SMEM)


def pack_kernel(plan_in, count_in, pages, out, plan, count, used, tags, sem, small_sem):
    devices = out.shape[0]
    rows = pages.shape[1]
    moves = plan.shape[2]
    small = [
        pltpu.make_async_copy(plan_in, plan, small_sem.at[0]),
        pltpu.make_async_copy(count_in, count, small_sem.at[1]),
    ]
    for copy in small:
        copy.start()
    for d in range(devices):
        used[d] = 0
        for r in range(CAP):
            tags[d * CAP + r] = -1
    for copy in small:
        copy.wait()

    def page_copy(source, target, rank):
        place = pl.ds(pl.multiple_of(rank * rows, rows), rows)
        return pltpu.make_async_copy(pages.at[source], out.at[target, place], sem)

    def send(k, carry):
        @pl.when(k < count[0])
        def _():
            target = plan[1, 0, k]
            rank = used[target]
            used[target] = rank + 1
            tags[target * CAP + rank] = plan[2, 0, k]
            page_copy(plan[0, 0, k], target, rank).start()

        return carry

    lax.fori_loop(0, moves, send, 0)
    row_at = lax.broadcasted_iota(jnp.int32, (ROW, pages.shape[2]), 0)
    for d in range(devices):
        tile = jnp.full(row_at.shape, -1, jnp.int32)
        for r in range(CAP):
            tile = jnp.where(row_at == r, tags[d * CAP + r], tile)
        out[d, CAP * rows :] = tile.astype(jnp.float32).astype(out.dtype)

    def finish(k, carry):
        @pl.when(k < count[0])
        def _():
            page_copy(0, 0, 0).wait()

        return carry

    lax.fori_loop(0, moves, finish, 0)


def partials(q_groups, key_pages, value_pages, firsts, lengths, scale):
    scores = [
        lax.dot_general(
            q, k, (((1,), (1,)), ((), ())), preferred_element_type=jnp.float32
        )
        * scale
        for q, k in zip(q_groups, key_pages)
    ]
    position = lax.broadcasted_iota(jnp.int32, scores[0].shape, 1)
    scores = jnp.stack(
        [
            jnp.where(position < length - first, s, NEG)
            for s, first, length in zip(scores, firsts, lengths)
        ]
    )
    largest = jnp.max(scores, axis=2, keepdims=True)
    expo = jnp.exp(scores - largest)
    total = jnp.sum(expo, axis=2, keepdims=True)
    weights = expo.astype(jnp.bfloat16)
    mixed = jnp.stack(
        [
            jnp.dot(weights[n], v, preferred_element_type=jnp.float32)
            for n, v in enumerate(value_pages)
        ]
    )
    return (
        jnp.broadcast_to(largest, mixed.shape),
        jnp.broadcast_to(total, mixed.shape),
        mixed,
    )


def local_kernel(
    heads, scale, table, lens, query, pages, new_pages, mixed_out, top_out, sum_out, owner,
    held, read_sem, write_sem,
):
    slots = pages.shape[0]
    block = pages.shape[1] // (2 * heads)
    seqs, blocks = table.shape
    group = query.shape[1] // heads

    def read(i):
        return pltpu.make_async_copy(pages.at[i], held.at[i], read_sem.at[i])

    def write(i):
        return pltpu.make_async_copy(held.at[i], new_pages.at[i], write_sem)

    def start_read(i, carry):
        read(i).start()
        owner[i] = -1
        return carry

    lax.fori_loop(0, slots, start_read, 0)

    def own(i, carry):
        for b in range(blocks):
            owner[table[i, b]] = i * blocks + b
        return carry

    lax.fori_loop(0, seqs, own, 0)

    def pass_on(i, carry):
        read(i).wait()
        write(i).start()
        return carry

    lax.fori_loop(0, slots, pass_on, 0)

    def sequence(i, carry):
        q_rows = query[i].astype(jnp.float32)
        places = [(b, h) for b in range(blocks) for h in range(heads)]
        groups = [
            q_rows[h * group : (h + 1) * group].astype(jnp.bfloat16) for h in range(heads)
        ]
        slot = [table[i, b] for b in range(blocks)]
        found = partials(
            [groups[h] for b, h in places],
            [held[slot[b], 2 * h * block : (2 * h + 1) * block] for b, h in places],
            [held[slot[b], (2 * h + 1) * block : (2 * h + 2) * block] for b, h in places],
            [b * block for b, h in places],
            [lens[i]] * len(places),
            scale,
        )
        for ref, value in zip((top_out, sum_out, mixed_out), found):
            ref[pl.ds(i * blocks, blocks)] = value.reshape(blocks, heads * group, -1)
        return carry

    lax.fori_loop(0, seqs, sequence, 0)

    def finish(i, carry):
        write(i).wait()
        return carry

    lax.fori_loop(0, slots, finish, 0)


def final_kernel(
    heads, scale, copies, lens, owner, query, arrived_in, mixed_in, top_in, sum_in, pages_in,
    pages_out, out, arrived, mixed, top, total, tags, sem, in_sem, tag_sem, page_sem,
):
    devices = arrived.shape[0]
    rows = pages_out.shape[1]
    block = rows // (2 * heads)
    seqs = query.shape[0]
    entries = mixed_in.shape[0]
    blocks = entries // seqs
    group = query.shape[1] // heads
    lanes = query.shape[2]
    tag_rows = pl.ds(CAP * rows, ROW)
    page_rows = pl.ds(0, CAP * rows)
    tag_copy = pltpu.make_async_copy(arrived_in.at[:, tag_rows], arrived.at[:, tag_rows], tag_sem)
    tag_copy.start()
    bring = [
        pltpu.make_async_copy(arrived_in.at[d, page_rows], arrived.at[d, page_rows], page_sem.at[d])
        for d in range(devices)
    ]
    for copy in bring:
        copy.start()
    fetch = [
        pltpu.make_async_copy(source, target.at[pl.ds(0, entries)], in_sem.at[n])
        for n, (source, target) in enumerate(((mixed_in, mixed), (top_in, top), (sum_in, total)))
    ]
    for copy in fetch:
        copy.start()

    tag_copy.wait()
    row_at = lax.broadcasted_iota(jnp.int32, (ROW, lanes), 0)
    for d in range(devices):
        tile = arrived[d, CAP * rows :].astype(jnp.float32)
        for r in range(CAP):
            tags[d * CAP + r] = jnp.max(jnp.where(row_at == r, tile, -1.0)).astype(jnp.int32)

    def place(d, r, slot):
        return pltpu.make_async_copy(
            arrived.at[d, pl.ds(r * rows, rows)], pages_out.at[slot], sem
        )

    for d in range(devices):
        bring[d].wait()
        for r in range(CAP):
            @pl.when(tags[d * CAP + r] >= 0)
            def _():
                place(d, r, tags[d * CAP + r]).start()

    for copy in fetch:
        copy.wait()

    def renew(sources):
        pairs = [(d, r) for d in sources for r in range(CAP)]
        q_groups, keys, values, firsts, lengths, targets = [], [], [], [], [], []
        for d, r in pairs:
            slot = tags[d * CAP + r]
            entry = jnp.where(slot >= 0, owner[jnp.maximum(slot, 0)], -1)
            at = jnp.maximum(entry, 0)
            i = at // blocks
            targets.append(jnp.where(entry >= 0, entry, entries))
            q_rows = query[i].astype(jnp.float32)
            for h in range(heads):
                q_groups.append(q_rows[h * group : (h + 1) * group].astype(jnp.bfloat16))
                start = r * rows + 2 * h * block
                keys.append(arrived[d, start : start + block])
                values.append(arrived[d, start + block : start + 2 * block])
                firsts.append((at - i * blocks) * block)
                lengths.append(lens[i])
        found = partials(q_groups, keys, values, firsts, lengths, scale)
        for ref, value in zip((top, total, mixed), found):
            pages_value = value.reshape(len(pairs), heads * group, lanes)
            for n, target in enumerate(targets):
                ref[target] = pages_value[n]

    if devices <= 8:
        renew(range(devices))
    else:
        lax.fori_loop(0, devices, lambda d, c: (renew([d]), c)[1], 0)

    for i in range(seqs):
        mine = pl.ds(i * blocks, blocks)
        largest = top[mine]
        factor = jnp.exp(largest - jnp.max(largest, axis=0, keepdims=True))
        value = jnp.sum(mixed[mine] * factor, axis=0) / jnp.sum(total[mine] * factor, axis=0)
        value = value.astype(out.dtype)
        for c in range(copies):
            out[c, i] = value

    for d in range(devices):
        for r in range(CAP):
            @pl.when(tags[d * CAP + r] >= 0)
            def _():
                place(d, r, 0).wait()


def exchange_sum(value, size):
    me = lax.axis_index("tensor")
    pairs = lambda bit: [(i, i ^ bit) for i in range(size)]
    half = value.shape[0] // 2
    low = (me % 2) == 0
    travel = value.astype(jnp.bfloat16)
    given = jnp.where(low, travel[half:], travel[:half])
    kept = jnp.where(low, value[:half], value[half:])
    total = kept + lax.ppermute(given, "tensor", pairs(1)).astype(jnp.float32)
    bit = 2
    while bit < size:
        total = total + lax.ppermute(
            total.astype(jnp.bfloat16), "tensor", pairs(bit)
        ).astype(jnp.float32)
        bit *= 2
    mine = total.astype(jnp.bfloat16)
    other = lax.ppermute(mine, "tensor", pairs(1))
    return jnp.concatenate([jnp.where(low, mine, other), jnp.where(low, other, mine)])


def body(query, kv_pages, move_plan, move_count, block_table, seq_lens, out_weight):
    slots, heads, two, block, lanes = kv_pages.shape
    seqs, local_q, _ = query.shape
    devices = lax.axis_size("dp")
    tensor = lax.axis_size("tensor")
    blocks = block_table.shape[1]
    group = local_q // heads
    rows = heads * two * block
    scale = 1.0 / math.sqrt(lanes)
    pages = kv_pages.reshape(slots, rows, lanes)
    plan = jnp.transpose(move_plan, (1, 0, 2))

    outgoing = pl.pallas_call(
        pack_kernel,
        out_shape=jax.ShapeDtypeStruct((devices, CAP * rows + ROW, lanes), kv_pages.dtype),
        in_specs=[ANY, ANY, ANY],
        out_specs=VMEM,
        scratch_shapes=[
            pltpu.SMEM(plan.shape, jnp.int32),
            pltpu.SMEM((1,), jnp.int32),
            pltpu.SMEM((devices,), jnp.int32),
            pltpu.SMEM((devices * CAP,), jnp.int32),
            pltpu.SemaphoreType.DMA,
            pltpu.SemaphoreType.DMA((2,)),
        ],
        name="pack",
    )(plan, move_count, pages)
    arrived = lax.all_to_all(outgoing, "dp", split_axis=0, concat_axis=0, tiled=True)

    entries = seqs * blocks
    part_shape = jax.ShapeDtypeStruct((entries, local_q, lanes), jnp.float32)
    part_scratch = pltpu.VMEM((entries + 1, local_q, lanes), jnp.float32)
    copied, mixed, top, total, owner = pl.pallas_call(
        functools.partial(local_kernel, heads, scale),
        out_shape=(
            jax.ShapeDtypeStruct(pages.shape, pages.dtype),
            part_shape,
            part_shape,
            part_shape,
            jax.ShapeDtypeStruct((slots,), jnp.int32),
        ),
        in_specs=[SMEM, SMEM, VMEM, ANY],
        out_specs=(ANY, VMEM, VMEM, VMEM, SMEM),
        scratch_shapes=[
            pltpu.VMEM(pages.shape, pages.dtype),
            pltpu.SemaphoreType.DMA((slots,)),
            pltpu.SemaphoreType.DMA,
        ],
        name="local",
        cost_estimate=pl.CostEstimate(
            flops=4 * seqs * blocks * local_q * block * lanes,
            bytes_accessed=4 * slots * rows * lanes,
            transcendentals=0,
        ),
        compiler_params=pltpu.CompilerParams(vmem_limit_bytes=24 << 20),
    )(block_table, seq_lens, query, pages)

    new_pages, attention = pl.pallas_call(
        functools.partial(final_kernel, heads, scale, devices),
        out_shape=(
            jax.ShapeDtypeStruct(pages.shape, pages.dtype),
            jax.ShapeDtypeStruct((devices, seqs, local_q, lanes), jnp.bfloat16),
        ),
        in_specs=[SMEM, SMEM, VMEM, ANY, ANY, ANY, ANY, ANY],
        out_specs=(ANY, VMEM),
        scratch_shapes=[
            pltpu.VMEM(arrived.shape, arrived.dtype),
            part_scratch,
            part_scratch,
            part_scratch,
            pltpu.SMEM((devices * CAP,), jnp.int32),
            pltpu.SemaphoreType.DMA,
            pltpu.SemaphoreType.DMA((3,)),
            pltpu.SemaphoreType.DMA,
            pltpu.SemaphoreType.DMA((devices,)),
        ],
        input_output_aliases={7: 0},
        name="final",
        compiler_params=pltpu.CompilerParams(vmem_limit_bytes=24 << 20),
    )(seq_lens, owner, query, arrived, mixed, top, total, copied)

    every = lax.all_to_all(attention, "dp", split_axis=0, concat_axis=0, tiled=True)
    partial_sums = jnp.dot(
        every.reshape(devices * seqs, local_q * lanes),
        out_weight,
        preferred_element_type=jnp.float32,
    )
    summed = exchange_sum(partial_sums, tensor)
    return (new_pages.reshape(kv_pages.shape), summed)


def solution(mesh):
    placed = (
        P("dp", "tensor", None),
        P("dp", "tensor", None, None, None),
        P("dp", None, None),
        P("dp"),
        P("dp", None),
        P("dp"),
        P("tensor", "dp"),
    )
    return jax.shard_map(
        body,
        mesh=mesh,
        in_specs=placed,
        out_specs=(P("dp", "tensor", None, None, None), P(None, "dp")),
        check_vma=False,
    )
```

time: 102 us -> 88.9 us (0.87)
  Pallas kernels: 57.5 us -> 26.3 us
  waiting for transfers between devices: 23.2 us -> 38.6 us
  local copies, waits for them, and re-layouts: 2.59 us -> 5.47 us
    pallas_call x1, Pallas kernels: 39.7 us -> 19.9 us  [body(): pl.pallas_call(functools.partial(local_kernel, heads, scale), out_shape=(...]
    all_to_all x1, waiting for transfers between devices: 8.84 us -> 24.2 us  [body(): lax.all_to_all(outgoing, 'dp', split_axis=0, concat_axis=0, tiled=True)]
    pallas_call x1, Pallas kernels: 14.3 us -> 2.88 us  [body(): pl.pallas_call(functools.partial(final_kernel, heads, scale, devices), ou...]
    unnamed x3 -> x12, local copies, waits for them, and re-layouts: 2.59 us -> 5.47 us
  transfers between devices with their start and end apart: 5 -> 5, of which waited for: 5 -> 5; matrix products, arithmetic and copies ran while one was open for 0% -> 0% of each run, Pallas kernels for 39% -> 23%
where the time goes in v2:
time: 88.9 us; the launch traced here: 88.4 us
  waiting for transfers between devices  38.6 us (43%)
  Pallas kernels  26.3 us (30%)
  starting transfers between devices  12.8 us (14%)
  local copies, waits for them, and re-layouts  5.47 us (6%)
  matrix products  3.03 us (3%)
  between operations  1.41 us (2%)
    all_to_all x1, waiting for transfers between devices, body(): lax.all_to_all(outgoing, 'dp', split_axis=0, concat_axis=0, tiled=True)  24.2 us
    pallas_call x1, Pallas kernels, body(): pl.pallas_call(functools.partial(local_kernel, heads, scale), out_shape=(...  19.9 us
    all_to_all x1, waiting for transfers between devices, body(): lax.all_to_all(attention, 'dp', split_axis=0, concat_axis=0, tiled=True)  9.1 us
    all_to_all x1, starting transfers between devices, body(): lax.all_to_all(outgoing, 'dp', split_axis=0, concat_axis=0, tiled=True)  7.5 us
    unnamed x12, local copies, waits for them, and re-layouts  5.47 us
    all_to_all x1, starting transfers between devices, body(): lax.all_to_all(attention, 'dp', split_axis=0, concat_axis=0, tiled=True)  3.65 us
    pallas_call x1, Pallas kernels, body(): pl.pallas_call(pack_kernel, out_shape=jax.ShapeDtypeStruct((devices, CAP...  3.52 us
    dot_general x1, matrix products, body(): jnp.dot(every.reshape(devices * seqs, local_q * lanes), out_weight, prefe...  3.03 us
  transfers between devices with their start and end apart: 5, of which 5 were waited for; matrix products, arithmetic and copies ran while one was open for 0% of the time, Pallas kernels for 23%

profile of v2, /device:TPU:0, one launch (start us, length us, event | category | flops | bytes accessed | tf_op | source)
XLA Modules:
  0.0 88.4 jit_solution(15402167838502072481)
XLA Ops:
  1.3 3.5 %pack.1 = bf16[8,1032,128]{2,1,0:T(8,128)(2,1)} custom-call(s32[3,1,12]{2,1,0:T(1,128)} %bitcast.14, s32[1]{0:T(128)S(6)} %copy.18.count_in, bf16[70,512,128]{2,1,0:T(8,128)(2,1)} %bitcast.11), custom_call_target="tpu_custom_call" | custom-call | tf_op jit(solution)/shard_map/pack/pallas_call | solution.py:293
  4.8 0.0 copy-start.3
  4.8 0.0 copy-start.4
  4.8 0.0 copy-start.5
  4.8 7.5 %all-to-all-start = ((bf16[8,1032,128]{2,1,0:T(8,128)(2,1)}), bf16[8,1032,128]{2,1,0:T(8,128)(2,1)S(1)}, u32[]{:S(2)}, u32[]{:S(2)}) async-start(bf16[8,1032,128]{2,1,0:T(8,128)(2,1)} %pack.1), calls=%async_computation | async-start | bytes 4227072 | tf_op jit(solution)/shard_map/all_to_all | solution.py:308
  12.3 0.0 copy-done.3
  12.3 0.0 copy-done.4
  12.4 0.0 copy-done.5
  12.4 0.0 copy-start
  12.4 3.6 %copy-done = bf16[70,2,2,128,128]{4,3,2,1,0:T(8,128)(2,1)S(1)} copy-done((bf16[70,2,2,128,128]{4,3,2,1,0:T(8,128)(2,1)S(1)}, bf16[70,2,2,128,128]{4,3,2,1,0:T(8,128)(2,1)}, u32[]{:S(2)}) %copy-start) | copy-done | bytes 9175064
  16.0 19.9 %local.1 = (bf16[70,512,128]{2,1,0:T(8,128)(2,1)}, f32[64,16,128]{2,1,0:T(8,128)S(1)}, f32[64,16,128]{2,1,0:T(8,128)S(1)}, f32[64,16,128]{2,1,0:T(8,128)S(1)}, s32[70]{0:T(128)S(1)}) custom-call(s32[8,8]{1,0:T(8,128)S(1)} %copy-done.4, s32[8]{0:T(128)S(1)} %copy-done.5, bf16[8,16,128]{2,1,0:T(8,128)(2,1)S(1)} %copy-done.3, bf16[70,512,128]{2,1,0:T(8,128)(2,1)S(1)} %bitcast.12), custom_call_target="tpu_custom_call" | custom-call | flops 67108864 | bytes 18350080 | tf_op jit(solution)/shard_map/local/pallas_call | solution.py:313
  35.9 0.0 copy-start.1
  35.9 0.8 copy-done.1
  36.7 24.2 %all-to-all-done.arrived_in = bf16[8,1032,128]{2,1,0:T(8,128)(2,1)S(1)} async-done(((bf16[8,1032,128]{2,1,0:T(8,128)(2,1)}), bf16[8,1032,128]{2,1,0:T(8,128)(2,1)S(1)}, u32[]{:S(2)}, u32[]{:S(2)}) %all-to-all-start) | async-done | bytes 2113568 | tf_op jit(solution)/shard_map/all_to_all | solution.py:308
  60.9 0.0 copy-start.2
  60.9 1.0 %copy-done.2 = f32[64,16,128]{2,1,0:T(8,128)S(1)} copy-done((f32[64,16,128]{2,1,0:T(8,128)S(1)}, f32[64,16,128]{2,1,0:T(8,128)}, u32[]{:S(2)}) %copy-start.2) | copy-done | bytes 524312
  62.0 2.9 %final.1 = (bf16[70,512,128]{2,1,0:T(8,128)(2,1)}, bf16[8,8,16,128]{3,2,1,0:T(8,128)(2,1)}) custom-call(s32[8]{0:T(128)S(1)} %copy-done.5, s32[70]{0:T(128)S(1)} %get-tuple-element.9.owner, bf16[8,16,128]{2,1,0:T(8,128)(2,1)S(1)} %copy-done.3, bf16[8,1032,128]{2,1,0:T(8,128)(2,1)S(1)} %all-to-all-done.arrived_in, ...), custom_call_target="tpu_custom_call", output_to_operand_aliasing={{0}: (7, {})} | custom-call | tf_op jit(solution)/shard_map/final/pallas_call | solution.py:338
  64.9 3.6 %all-to-all-start.1 = ((bf16[8,8,16,128]{3,2,1,0:T(8,128)(2,1)}), bf16[8,8,16,128]{3,2,1,0:T(8,128)(2,1)S(1)}, u32[]{:S(2)}, u32[]{:S(2)}) async-start(bf16[8,8,16,128]{3,2,1,0:T(8,128)(2,1)} %get-tuple-element.15), calls=%async_computation.1 | async-start | bytes 524288 | tf_op jit(solution)/shard_map/all_to_all | solution.py:362
  68.5 9.1 %all-to-all-done.1 = bf16[8,8,16,128]{3,2,1,0:T(8,128)(2,1)S(1)} async-done(((bf16[8,8,16,128]{3,2,1,0:T(8,128)(2,1)}), bf16[8,8,16,128]{3,2,1,0:T(8,128)(2,1)S(1)}, u32[]{:S(2)}, u32[]{:S(2)}) %all-to-all-start.1) | async-done | bytes 262176 | tf_op jit(solution)/shard_map/all_to_all | solution.py:362
  77.6 3.0 %fusion.5 = (bf16[64,1024]{1,0:T(8,128)(2,1)S(1)}, f32[64,1024]{1,0:T(8,128)S(1)}) fusion(bf16[2048,1024]{1,0:T(8,128)(2,1)} %param.13, bf16[8,8,16,128]{3,2,1,0:T(8,128)(2,1)S(1)} %all-to-all-done.1), kind=kOutput, calls=%fused_computation.11 | convolution fusion | flops 268500992 | bytes 4849664 | tf_op jit(solution)/shard_map/dot_general | solution.py:363
  80.7 0.1 collective-permute-start
  80.7 1.2 %collective-permute-done = bf16[32,1024]{1,0:T(8,128)(2,1)S(1)} collective-permute-done((bf16[32,1024]{1,0:T(8,128)(2,1)S(1)}, bf16[32,1024]{1,0:T(8,128)(2,1)S(1)}, u32[]{:S(2)}, u32[]{:S(2)}) %collective-permute-start) | collective-permute-done | bytes 65568 | tf_op jit(solution)/shard_map/ppermute | solution.py:269
  82.0 1.6 %collective-permute-start.1 = (bf16[32,1024]{1,0:T(8,128)(2,1)S(1)}, bf16[32,1024]{1,0:T(8,128)(2,1)S(1)}, u32[]{:S(2)}, u32[]{:S(2)}) collective-permute-start(bf16[32,1024]{1,0:T(8,128)(2,1)S(1)} %fusion.4), channel_id=1, source_target_pairs={{0,2},{1,3},{2,0},{3,1},{4,6},{5,7},{6,4},{7,5},{8,10},{9,11},{10,... | collective-permute-start | bytes 196616 | tf_op jit(solution)/shard_map/ppermute | solution.py:272
  83.6 2.8 %collective-permute-done.1 = bf16[32,1024]{1,0:T(8,128)(2,1)S(1)} collective-permute-done((bf16[32,1024]{1,0:T(8,128)(2,1)S(1)}, bf16[32,1024]{1,0:T(8,128)(2,1)S(1)}, u32[]{:S(2)}, u32[]{:S(2)}) %collective-permute-start.1) | collective-permute-done | bytes 65568 | tf_op jit(solution)/shard_map/ppermute | solution.py:272
  86.4 0.1 collective-permute-start.2
  86.5 1.2 %collective-permute-done.2 = bf16[32,1024]{1,0:T(8,128)(2,1)S(1)} collective-permute-done((bf16[32,1024]{1,0:T(8,128)(2,1)S(1)}, bf16[32,1024]{1,0:T(8,128)(2,1)S(1)}, u32[]{:S(2)}, u32[]{:S(2)}) %collective-permute-start.2) | collective-permute-done | bytes 65568 | tf_op jit(solution)/shard_map/ppermute | solution.py:277
  87.7 0.7 pad_maximum_fusion
  (4 shorter events, 0.1 us)
Async XLA Ops:
  4.8 7.5 %copy-start.3 = (bf16[8,16,128]{2,1,0:T(8,128)(2,1)S(1)}, bf16[8,16,128]{2,1,0:T(8,128)(2,1)}, u32[]{:S(2)}) copy-start(bf16[8,16,128]{2,1,0:T(8,128)(2,1)} %query.3) | copy-start | bytes 98308
  4.8 7.5 %copy-start.4 = (s32[8,8]{1,0:T(8,128)S(1)}, s32[8,8]{1,0:T(8,128)}, u32[]{:S(2)}) copy-start(s32[8,8]{1,0:T(8,128)} %table.1) | copy-start | bytes 772
  4.8 7.5 %copy-start.5 = (s32[8]{0:T(128)S(1)}, s32[8]{0:T(128)}, u32[]{:S(2)}) copy-start(s32[8]{0:T(128)} %lens.3) | copy-start | bytes 100
  4.8 56.1 %all-to-all-start = ((bf16[8,1032,128]{2,1,0:T(8,128)(2,1)}), bf16[8,1032,128]{2,1,0:T(8,128)(2,1)S(1)}, u32[]{:S(2)}, u32[]{:S(2)}) async-start(bf16[8,1032,128]{2,1,0:T(8,128)(2,1)} %pack.1), calls=%async_computation | async-start | bytes 4227072 | tf_op jit(solution)/shard_map/all_to_all | solution.py:308
  12.4 3.6 %copy-start = (bf16[70,2,2,128,128]{4,3,2,1,0:T(8,128)(2,1)S(1)}, bf16[70,2,2,128,128]{4,3,2,1,0:T(8,128)(2,1)}, u32[]{:S(2)}) copy-start(bf16[70,2,2,128,128]{4,3,2,1,0:T(8,128)(2,1)} %param.8) | copy-start | bytes 27525124
  35.9 0.8 copy-start.1
  60.9 1.0 %copy-start.2 = (f32[64,16,128]{2,1,0:T(8,128)S(1)}, f32[64,16,128]{2,1,0:T(8,128)}, u32[]{:S(2)}) copy-start(f32[64,16,128]{2,1,0:T(8,128)} %copy-done.1) | copy-start | bytes 1572868
  64.9 12.7 %all-to-all-start.1 = ((bf16[8,8,16,128]{3,2,1,0:T(8,128)(2,1)}), bf16[8,8,16,128]{3,2,1,0:T(8,128)(2,1)S(1)}, u32[]{:S(2)}, u32[]{:S(2)}) async-start(bf16[8,8,16,128]{3,2,1,0:T(8,128)(2,1)} %get-tuple-element.15), calls=%async_computation.1 | async-start | bytes 524288 | tf_op jit(solution)/shard_map/all_to_all | solution.py:362
  80.7 1.3 %collective-permute-start = (bf16[32,1024]{1,0:T(8,128)(2,1)S(1)}, bf16[32,1024]{1,0:T(8,128)(2,1)S(1)}, u32[]{:S(2)}, u32[]{:S(2)}) collective-permute-start(bf16[32,1024]{1,0:T(8,128)(2,1)S(1)} %slice_select_fusion.1), channel_id=1, source_target_pairs={{0,1},{1,0},{2,3},{3,2},{4,5},{5,4},{6,7},{7,6},{8,9},{9,8},{10,11... | collective-permute-start | bytes 196616 | tf_op jit(solution)/shard_map/ppermute | solution.py:269
  82.0 4.3 %collective-permute-start.1 = (bf16[32,1024]{1,0:T(8,128)(2,1)S(1)}, bf16[32,1024]{1,0:T(8,128)(2,1)S(1)}, u32[]{:S(2)}, u32[]{:S(2)}) collective-permute-start(bf16[32,1024]{1,0:T(8,128)(2,1)S(1)} %fusion.4), channel_id=1, source_target_pairs={{0,2},{1,3},{2,0},{3,1},{4,6},{5,7},{6,4},{7,5},{8,10},{9,11},{10,... | collective-permute-start | bytes 196616 | tf_op jit(solution)/shard_map/ppermute | solution.py:272
  86.4 1.3 %collective-permute-start.2 = (bf16[32,1024]{1,0:T(8,128)(2,1)S(1)}, bf16[32,1024]{1,0:T(8,128)(2,1)S(1)}, u32[]{:S(2)}, u32[]{:S(2)}) collective-permute-start(bf16[32,1024]{1,0:T(8,128)(2,1)S(1)} %add_convert_fusion), channel_id=1, source_target_pairs={{0,1},{1,0},{2,3},{3,2},{4,5},{5,4},{6,7},{7,6},{8,9},{9,8},{10,11... | collective-permute-start | bytes 196616 | tf_op jit(solution)/shard_map/ppermute | solution.py:277
